TPU v7x, 32 devices: a whole 2x2x4 slice. The times are simulated.
32 devices in a mesh: row: 8 (over z, x), col: 4 (over y, core).
Axes of the slice: x: 2, y: 2, z: 4, core: 2. Of those that a mesh axis runs over, the one named last changes fastest.
Arguments:
- solution_field: float32 [32, 32768], P(None, ('row', 'col')), may hold values from -6 to 6
- residual: float32 [32, 32768], P(None, ('row', 'col')), may hold values from -420 to 420
- direction: float32 [32, 32768], P(None, ('row', 'col')), may hold values from -420 to 420
- positions: bfloat16 [2, 32768], P(None, ('row', 'col')), may hold values from -6 to 6
- tile_pairs: int32 [2, 49152], P(None, ('row', 'col')), may hold values from 0 to 63, as said below
- pair_count: int32 [32], P(('row', 'col')), may hold values from 0 to 1536, as said below
Outputs:
- solution_next: float32 [32, 32768], P(None, ('row', 'col'))
- residual_next: float32 [32, 32768], P(None, ('row', 'col'))
- direction_next: float32 [32, 32768], P(None, ('row', 'col'))
Inputs may be any that keep to these rules, and one draw needn't show every extreme that they name: `tile_pairs`: row 0 holds local row tiles below 32, row 1 local column tiles below 64. The live pairs of one slot block are distinct and strictly upper (I < J); entries in slots that are not live are in range but carry nothing. `pair_count`: some slot block is full in every draw.
All inputs are finite; a program needn't handle non-finite values.
Results may differ from a plain program's by a relative error of at most 0.007.
Values may be sent and summed in bfloat16 or wider, within the bound.
A program may use at most 64 MiB of HBM per device.

v0:
```python
import math
import jax
import jax.numpy as jnp
from jax import lax
from jax.sharding import PartitionSpec as P

TILE = 128
AMPLITUDE = 0.025
NUGGET = 2.0
RADIUS = 1.0
HIGHEST = lax.Precision.HIGHEST


def kernel_tile(near_side, far_side):
    differ = near_side[..., :, None] - far_side[..., None, :]
    distance = jnp.sqrt(jnp.sum(differ * differ, axis=0)) / RADIUS
    remain = jnp.maximum(1.0 - distance, 0.0)
    return AMPLITUDE * remain**4 * (4.0 * distance + 1.0)


def cross_gram_matrix(former, latter):
    return lax.dot_general(
        former,
        latter,
        (((1,), (1,)), ((), ())),
        precision=HIGHEST,
        preferred_element_type=jnp.float32,
    )


def apply_left(matrix, vectors):
    return jnp.dot(matrix.T, vectors, precision=HIGHEST)


def symmetric_solve(matrix, target):
    balanced = 0.5 * (matrix + matrix.T)
    factor = jnp.linalg.cholesky(balanced)
    middle = lax.linalg.triangular_solve(factor, target, left_side=True, lower=True)
    return lax.linalg.triangular_solve(factor, middle, left_side=True, lower=True, transpose_a=True)


def on_device(solution_field, residual, direction, positions, tile_pairs, pair_count):
    probes, own_points = direction.shape
    own_tiles = own_points // TILE
    dir_half = direction.astype(jnp.bfloat16)
    row_dir, row_pos = (
        lax.all_gather(dir_half, "col", axis=1, tiled=True),
        lax.all_gather(positions, "col", axis=1, tiled=True),
    )
    col_dir, col_pos = (
        lax.all_gather(dir_half, "row", axis=1, tiled=True),
        lax.all_gather(positions, "row", axis=1, tiled=True),
    )
    own_pos = positions.astype(jnp.float32).reshape(2, own_tiles, TILE)
    diagonal = kernel_tile(own_pos, own_pos).astype(jnp.bfloat16)
    own_product = jnp.einsum(
        "npq,knq->knp",
        diagonal,
        dir_half.reshape(probes, own_tiles, TILE),
        preferred_element_type=jnp.float32,
    ).reshape(probes, own_points)
    row_tiles = row_dir.shape[1] // TILE
    col_tiles = col_dir.shape[1] // TILE
    row_vector = row_dir.reshape(probes, row_tiles, TILE)
    column_vector = col_dir.reshape(probes, col_tiles, TILE)
    row_coord = row_pos.reshape(2, row_tiles, TILE)
    col_coord = col_pos.reshape(2, col_tiles, TILE)
    row_range = jnp.arange(row_tiles, dtype=jnp.int32)
    col_range = jnp.arange(col_tiles, dtype=jnp.int32)
    slot_total = tile_pairs.shape[1]
    block_size = math.gcd(slot_total, 64)
    live_count = pair_count[0]

    def stepped(block_no, running_totals):
        row_acc, col_acc = running_totals
        first_slot = block_no * block_size
        row_index = lax.dynamic_slice_in_dim(tile_pairs[0], first_slot, block_size)
        col_index = lax.dynamic_slice_in_dim(tile_pairs[1], first_slot, block_size)
        live_mask = first_slot + jnp.arange(block_size, dtype=jnp.int32) < live_count
        row_chosen_index = (row_index[:, None] == row_range[None, :]).astype(jnp.bfloat16)
        column_chosen_index = (col_index[:, None] == col_range[None, :]).astype(jnp.bfloat16)
        near_side = jnp.einsum(
            "bt,ctq->cbq", row_chosen_index, row_coord, preferred_element_type=jnp.float32
        )
        far_side = jnp.einsum(
            "bt,ctq->cbq", column_chosen_index, col_coord, preferred_element_type=jnp.float32
        )
        row_sel = jnp.einsum(
            "di,siz->sdz", row_chosen_index, row_vector, preferred_element_type=jnp.float32
        ).astype(jnp.bfloat16)
        col_sel = jnp.einsum(
            "di,siz->sdz", column_chosen_index, column_vector, preferred_element_type=jnp.float32
        ).astype(jnp.bfloat16)
        kernel_block = kernel_tile(near_side, far_side)
        kernel_block = jnp.where(live_mask[:, None, None], kernel_block, 0.0).astype(jnp.bfloat16)
        forward_step = jnp.einsum(
            "bpq,kbq->kbp", kernel_block, col_sel, preferred_element_type=jnp.float32
        )
        backward = jnp.einsum(
            "bpq,kbp->kbq", kernel_block, row_sel, preferred_element_type=jnp.float32
        )
        row_add = jnp.einsum(
            "bt,kbp->ktp",
            row_chosen_index.astype(jnp.float32),
            forward_step,
            precision=HIGHEST,
            preferred_element_type=jnp.float32,
        )
        col_add = jnp.einsum(
            "au,lax->lux",
            column_chosen_index.astype(jnp.float32),
            backward,
            precision=HIGHEST,
            preferred_element_type=jnp.float32,
        )
        return (row_acc + row_add, col_acc + col_add)

    start_totals = (
        jnp.zeros((probes, row_tiles, TILE), jnp.float32),
        jnp.zeros((probes, col_tiles, TILE), jnp.float32),
    )
    row_acc, col_acc = lax.fori_loop(0, slot_total // block_size, stepped, start_totals)
    row_flat = row_acc.reshape(probes, row_tiles * TILE)
    col_flat = col_acc.reshape(probes, col_tiles * TILE)
    row_whole = lax.psum(row_flat.astype(jnp.bfloat16), "col").astype(jnp.float32)
    row_part = lax.dynamic_slice_in_dim(
        row_whole, lax.axis_index("col") * own_points, own_points, 1
    )
    col_whole = lax.psum(col_flat.astype(jnp.bfloat16), "row").astype(jnp.float32)
    col_part = lax.dynamic_slice_in_dim(
        col_whole, lax.axis_index("row") * own_points, own_points, 1
    )
    applied = NUGGET * direction + own_product + row_part + col_part
    curvature, crossing, norm_old, image_resid, square = lax.psum(
        (
            cross_gram_matrix(direction, applied),
            cross_gram_matrix(direction, residual),
            cross_gram_matrix(residual, residual),
            cross_gram_matrix(applied, residual),
            cross_gram_matrix(applied, applied),
        ),
        ("row", "col"),
    )
    step_size = symmetric_solve(curvature, crossing)
    residual_next = residual - apply_left(step_size, applied)
    shifted = jnp.dot(step_size.T, image_resid, precision=HIGHEST)
    quadratic = jnp.dot(
        step_size.T, jnp.dot(square, step_size, precision=HIGHEST), precision=HIGHEST
    )
    norm_new = norm_old - shifted - shifted.T + quadratic
    solution_next = solution_field + apply_left(step_size, direction)
    mix_weight = symmetric_solve(norm_old, norm_new)
    direction_next = residual_next + apply_left(mix_weight, direction)
    return (solution_next, residual_next, direction_next)


def solution(mesh):
    in_specs = (
        P(None, ("row", "col")),
        P(None, ("row", "col")),
        P(None, ("row", "col")),
        P(None, ("row", "col")),
        P(None, ("row", "col")),
        P(("row", "col")),
    )
    out_specs = (P(None, ("row", "col")), P(None, ("row", "col")), P(None, ("row", "col")))
    return jax.shard_map(
        on_device, mesh=mesh, in_specs=in_specs, out_specs=out_specs, check_vma=False
    )
```

profile of v0, /device:TPU:0, one launch (start us, length us, event | category | flops | bytes accessed | tf_op | source)
XLA Modules:
  0.0 675.7 jit_solution(7881946723567846366)
XLA Ops:
  8.1 33.0 %all_gather.12 = bf16[32,8192]{1,0:T(8,128)(2,1)S(1)} all-gather(bf16[32,1024]{1,0:T(8,128)(2,1)S(1)} %convert_element_type.65), channel_id=1, replica_groups=mesh['row'=8,'col'=4] {'row'}, dimensions={1}, use_global_device_ids=true | all-gather | bytes 589824 | tf_op jit(solution)/shard_map/all_gather | solution.py:51
  41.2 5.8 all_gather.15
  46.9 30.7 %all_gather.14 = bf16[2,8192]{1,0:T(2,128)(2,1)S(1)} all-gather(bf16[2,1024]{1,0:T(2,128)(2,1)} %param.16), channel_id=1, replica_groups=mesh['row'=8,'col'=4] {'row'}, dimensions={1}, use_global_device_ids=true | all-gather | bytes 36864 | tf_op jit(solution)/shard_map/all_gather | solution.py:52
  77.7 5.3 all_gather.13
  84.0 413.3 %while.16 = (s32[]{:T(128)}, f32[32,32,128]{2,1,0:T(8,128)}, f32[32,64,128]{2,1,0:T(8,128)}, s32[2,1536]{1,0:T(2,128)}, bf16[32,64,128]{2,1,0:T(8,128)(2,1)}, /*...) while((s32[]{:T(128)}, f32[32,32,128]{2,1,0:T(8,128)}, ...), condition=%wide.region_3.4_spmd.clone, body=%wide.region_1.3_spmd.clone.sunk | while | flops 506742912 | bytes 25242432 | solution.py:122
  107.3 3.5 fusion.128
  113.4 3.0 fusion.126
  124.6 3.5 fusion.128
  141.9 3.5 fusion.128
  159.2 3.5 fusion.128
  176.5 3.5 fusion.128
  193.9 3.5 fusion.128
  211.2 3.5 fusion.128
  228.5 3.5 fusion.128
  245.8 3.5 fusion.128
  263.1 3.5 fusion.128
  280.4 3.5 fusion.128
  297.7 3.5 fusion.128
  315.1 3.5 fusion.128
  332.4 3.5 fusion.128
  349.7 3.5 fusion.128
  367.0 3.5 fusion.128
  384.3 3.5 fusion.128
  401.6 3.5 fusion.128
  418.9 3.5 fusion.128
  436.2 3.5 fusion.128
  453.6 3.5 fusion.128
  470.9 3.5 fusion.128
  488.2 3.5 fusion.128
  503.2 29.6 %all-reduce.4.cloned.1.call-done = bf16[32,4096]{1,0:T(8,128)(2,1)} async-done(((bf16[32,4096]{1,0:T(8,128)(2,1)}), bf16[32,4096]{1,0:T(8,128)(2,1)}) %all-reduce.4.cloned.1.call-update) | async-done | bytes 262160 | tf_op jit(solution)/shard_map/psum | solution.py:125
  532.8 76.2 %all-reduce.6.cloned.1.call-done = bf16[32,8192]{1,0:T(8,128)(2,1)} async-done(((bf16[32,8192]{1,0:T(8,128)(2,1)}), bf16[32,8192]{1,0:T(8,128)(2,1)}) %all-reduce.6.cloned.1.call-update) | async-done | bytes 524304 | tf_op jit(solution)/shard_map/psum | solution.py:129
  610.7 40.8 %all-reduce = (f32[32,32]{1,0:T(8,128)S(1)}, f32[32,32]{1,0:T(8,128)S(1)}, f32[32,32]{1,0:T(8,128)S(1)}, f32[32,32]{1,0:T(8,128)S(1)}, f32[32,32]{1,0:T(8,128)S(1)}) all-reduce(f32[32,32]{1,0:T(8,128)S(1)} %fusion.49, f32[32,32]{1,0:T(8,128)S(1)} %convolution_bitcast_fusion.7, ...), channel_id=1, replica_groups=mesh['row'=8,'col'=4] {'row','col'}, use_global_device_ids=true, to_apply=%region_9.0 | all-reduce | flops 5120 | bytes 40960 | tf_op jit(solution)/shard_map/psum | solution.py:134
  (351 shorter events, 354.4 us)
Async XLA Ops:
  7.2 525.6 %all-reduce.4.cloned.1.call-start = ((), (), s32[]{:S(2)}) async-start(), calls=%async_computation | async-start | bytes 524288 | tf_op jit(solution)/shard_map/psum | solution.py:125
  497.3 4.6 copy-start.4
  497.3 4.9 copy-start
  497.3 5.3 copy-start.1
  499.3 167.7 %copy-start.3 = (f32[32,1024]{1,0:T(8,128)S(1)}, f32[32,1024]{1,0:T(8,128)}, u32[]{:S(2)}) copy-start(f32[32,1024]{1,0:T(8,128)} %param.13) | copy-start | bytes 393220
  499.3 109.7 %all-reduce.6.cloned.1.call-start = ((), (), s32[]{:S(2)}) async-start(), calls=%async_computation.1 | async-start | bytes 1048576 | tf_op jit(solution)/shard_map/psum | solution.py:129
  665.9 3.0 copy-start.2
Sparse Core Ops, SparseCore 0:
  499.4 33.3 all-reduce.3
  536.2 72.7 all-reduce.5
where the time goes:
time: 681 us; the launch traced here: 676 us
  matrix products  255 us (37%)
  other arithmetic  159 us (23%)
  blocking collectives  116 us (17%)
  waiting for transfers between devices  106 us (16%)
  local copies, waits for them, and re-layouts  24.3 us (4%)
  between operations  14.3 us (2%)
    dot_general x24, matrix products, stepped(): jnp.einsum('au,lax->lux', column_chosen_index.astype(jnp.float32), backwa...  83.6 us
    psum x1, waiting for transfers between devices, on_device(): lax.psum(col_flat.astype(jnp.bfloat16), 'row').astype(jnp.float32)  76.2 us
    dot_general x24, matrix products, stepped(): jnp.einsum('bt,kbp->ktp', row_chosen_index.astype(jnp.float32), forward_s...  70.3 us
    reduce_sum x25, other arithmetic, kernel_tile(): distance = jnp.sqrt(jnp.sum(differ * differ, axis=0)) / RADIUS  66.6 us
    convert_element_type x24, other arithmetic, stepped(): jnp.where(live_mask[:, None, None], kernel_block, 0.0).astype(jnp.bfloat16)  59 us
    psum x1, blocking collectives, on_device(): lax.psum((cross_gram_matrix(direction, applied), cross_gram_matrix(direct...  40.8 us
    dot_general x24, matrix products, stepped(): jnp.einsum('di,siz->sdz', column_chosen_index, column_vector, preferred_e...  33.2 us
    all_gather x1, blocking collectives, on_device(): lax.all_gather(dir_half, 'row', axis=1, tiled=True)  33 us
  transfers between devices with their start and end apart: 2, of which 2 were waited for; matrix products, arithmetic and copies ran while one was open for 1% of the time, Pallas kernels for 0%

commit v1 on v0

--- a/solution.py
+++ b/solution.py
@@ -126,7 +126,9 @@
     row_part = lax.dynamic_slice_in_dim(
         row_whole, lax.axis_index("col") * own_points, own_points, 1
     )
-    col_whole = lax.psum(col_flat.astype(jnp.bfloat16), "row").astype(jnp.float32)
+    col_whole = jnp.sum(lax.all_gather(col_flat.astype(jnp.bfloat16), "row"), axis=0).astype(
+        jnp.float32
+    )
     col_part = lax.dynamic_slice_in_dim(
         col_whole, lax.axis_index("row") * own_points, own_points, 1
     )

time: 681 us -> 657 us (0.965)
  waiting for transfers between devices: 106 us -> 70.6 us
  local copies, waits for them, and re-layouts: 24.3 us -> 31.8 us
    psum x1 -> x0, waiting for transfers between devices: 76.2 us -> none  [on_device(): lax.psum(col_flat.astype(jnp.bfloat16), 'row').astype(jnp.float32)]
    all_gather x0 -> x1, waiting for transfers between devices: none -> 70.6 us  [on_device(): lax.all_gather(col_flat.astype(jnp.bfloat16), 'row')]
    psum x1, waiting for transfers between devices: 29.6 us -> 0.03 us  [on_device(): lax.psum(row_flat.astype(jnp.bfloat16), 'col').astype(jnp.float32)]
    while x0 -> x288, local copies, waits for them, and re-layouts: none -> 7.61 us
  transfers between devices with their start and end apart: 2 -> 2, of which waited for: 2 -> 1; matrix products, arithmetic and copies ran while one was open for 1% -> 1% of each run, Pallas kernels for 0% -> 0%
where the time goes in v1:
time: 657 us; the launch traced here: 652 us
  matrix products  255 us (39%)
  other arithmetic  162 us (25%)
  blocking collectives  115 us (18%)
  waiting for transfers between devices  70.6 us (11%)
  local copies, waits for them, and re-layouts  31.8 us (5%)
  between operations  15.8 us (2%)
    dot_general x24, matrix products, stepped(): jnp.einsum('au,lax->lux', column_chosen_index.astype(jnp.float32), backwa...  83.6 us
    all_gather x1, waiting for transfers between devices, on_device(): lax.all_gather(col_flat.astype(jnp.bfloat16), 'row')  70.6 us
    dot_general x24, matrix products, stepped(): jnp.einsum('bt,kbp->ktp', row_chosen_index.astype(jnp.float32), forward_s...  69.9 us
    reduce_sum x25, other arithmetic, kernel_tile(): distance = jnp.sqrt(jnp.sum(differ * differ, axis=0)) / RADIUS  66.6 us
    convert_element_type x24, other arithmetic, stepped(): jnp.where(live_mask[:, None, None], kernel_block, 0.0).astype(jnp.bfloat16)  59 us
    psum x1, blocking collectives, on_device(): lax.psum((cross_gram_matrix(direction, applied), cross_gram_matrix(direct...  40 us
    dot_general x24, matrix products, stepped(): jnp.einsum('di,siz->sdz', column_chosen_index, column_vector, preferred_e...  33.4 us
    all_gather x1, blocking collectives, on_device(): lax.all_gather(dir_half, 'row', axis=1, tiled=True)  33 us
  transfers between devices with their start and end apart: 2, of which 1 were waited for; matrix products, arithmetic and copies ran while one was open for 1% of the time, Pallas kernels for 0%

profile of v1, /device:TPU:0, one launch (start us, length us, event | category | flops | bytes accessed | tf_op | source)
XLA Modules:
  0.0 652.1 jit_solution(2233217710417401986)
XLA Ops:
  9.0 33.0 %all_gather.16 = bf16[32,8192]{1,0:T(8,128)(2,1)S(1)} all-gather(bf16[32,1024]{1,0:T(8,128)(2,1)S(1)} %convert_element_type.74), channel_id=1, replica_groups=mesh['row'=8,'col'=4] {'row'}, dimensions={1}, use_global_device_ids=true | all-gather | bytes 589824 | tf_op jit(solution)/shard_map/all_gather | solution.py:51
  42.0 5.8 all_gather.19
  47.8 30.7 %all_gather.18 = bf16[2,8192]{1,0:T(2,128)(2,1)S(1)} all-gather(bf16[2,1024]{1,0:T(2,128)(2,1)} %param.16), channel_id=1, replica_groups=mesh['row'=8,'col'=4] {'row'}, dimensions={1}, use_global_device_ids=true | all-gather | bytes 36864 | tf_op jit(solution)/shard_map/all_gather | solution.py:52
  78.5 5.3 all_gather.17
  84.8 421.4 %while.16 = (s32[]{:T(128)}, f32[32,32,128]{2,1,0:T(8,128)}, f32[32,64,128]{2,1,0:T(8,128)}, s32[2,1536]{1,0:T(2,128)}, bf16[32,64,128]{2,1,0:T(8,128)(2,1)}, /*...) while((s32[]{:T(128)}, f32[32,32,128]{2,1,0:T(8,128)}, ...), condition=%wide.region_3.4_spmd.clone, body=%wide.region_1.3_spmd.clone.sunk | while | flops 506742912 | bytes 25508840 | solution.py:122
  108.8 3.5 fusion.128
  114.9 3.0 fusion.126
  126.4 3.5 fusion.128
  132.6 3.0 fusion.126
  144.1 3.5 fusion.128
  161.7 3.5 fusion.128
  179.4 3.5 fusion.128
  197.0 3.5 fusion.128
  214.7 3.5 fusion.128
  232.3 3.5 fusion.128
  250.0 3.5 fusion.128
  267.6 3.5 fusion.128
  285.3 3.5 fusion.128
  302.9 3.5 fusion.128
  320.6 3.5 fusion.128
  338.2 3.5 fusion.128
  355.9 3.5 fusion.128
  373.5 3.5 fusion.128
  391.2 3.5 fusion.128
  408.8 3.5 fusion.128
  426.5 3.5 fusion.128
  444.1 3.5 fusion.128
  461.8 3.5 fusion.128
  479.4 3.5 fusion.128
  497.1 3.5 fusion.128
  512.1 70.6 %all-gather.2.cloned.1.call-done = bf16[8,32,8192]{2,1,0:T(8,128)(2,1)} async-done(((bf16[1,32,8192]{2,1,0:T(8,128)(2,1)}), bf16[8,32,8192]{2,1,0:T(8,128)(2,1)}) %all-gather.2.cloned.1.call-update) | async-done | bytes 4194320 | tf_op jit(solution)/shard_map/all_gather | solution.py:129
  587.2 40.0 %all-reduce = (f32[32,32]{1,0:T(8,128)S(1)}, f32[32,32]{1,0:T(8,128)S(1)}, f32[32,32]{1,0:T(8,128)S(1)}, f32[32,32]{1,0:T(8,128)S(1)}, f32[32,32]{1,0:T(8,128)S(1)}) all-reduce(f32[32,32]{1,0:T(8,128)S(1)} %fusion.49, f32[32,32]{1,0:T(8,128)S(1)} %convolution_bitcast_fusion.7, ...), channel_id=1, replica_groups=mesh['row'=8,'col'=4] {'row','col'}, use_global_device_ids=true, to_apply=%region_9.0 | all-reduce | flops 5120 | bytes 40960 | tf_op jit(solution)/shard_map/psum | solution.py:136
  (640 shorter events, 361.7 us)
Async XLA Ops:
  8.0 574.7 %all-gather.2.cloned.1.call-start = ((), (), s32[]{:S(2)}) async-start(), calls=%async_computation.1 | async-start | bytes 4718592 | tf_op jit(solution)/shard_map/all_gather | solution.py:129
  85.8 6.6 %copy-start.7 = (s32[64]{0:T(128)}, s32[64]{0:T(128)S(1)}, u32[]{:S(2)}) copy-start(s32[64]{0:T(128)S(1)} %get-tuple-element.318) | copy-start | bytes 772 | tf_op jit(solution)/shard_map/while
  101.1 6.6 %copy-start.7 = (s32[64]{0:T(128)}, s32[64]{0:T(128)S(1)}, u32[]{:S(2)}) copy-start(s32[64]{0:T(128)S(1)} %get-tuple-element.318) | copy-start | bytes 772 | tf_op jit(solution)/shard_map/while
  108.8 6.2 copy-start.8
  118.8 6.6 %copy-start.7 = (s32[64]{0:T(128)}, s32[64]{0:T(128)S(1)}, u32[]{:S(2)}) copy-start(s32[64]{0:T(128)S(1)} %get-tuple-element.318) | copy-start | bytes 772 | tf_op jit(solution)/shard_map/while
  126.4 6.2 copy-start.8
  136.4 6.6 %copy-start.7 = (s32[64]{0:T(128)}, s32[64]{0:T(128)S(1)}, u32[]{:S(2)}) copy-start(s32[64]{0:T(128)S(1)} %get-tuple-element.318) | copy-start | bytes 772 | tf_op jit(solution)/shard_map/while
  144.1 6.2 copy-start.8
  154.1 6.6 %copy-start.7 = (s32[64]{0:T(128)}, s32[64]{0:T(128)S(1)}, u32[]{:S(2)}) copy-start(s32[64]{0:T(128)S(1)} %get-tuple-element.318) | copy-start | bytes 772 | tf_op jit(solution)/shard_map/while
  161.7 6.2 copy-start.8
  171.7 6.6 %copy-start.7 = (s32[64]{0:T(128)}, s32[64]{0:T(128)S(1)}, u32[]{:S(2)}) copy-start(s32[64]{0:T(128)S(1)} %get-tuple-element.318) | copy-start | bytes 772 | tf_op jit(solution)/shard_map/while
  179.4 6.2 copy-start.8
  189.4 6.6 %copy-start.7 = (s32[64]{0:T(128)}, s32[64]{0:T(128)S(1)}, u32[]{:S(2)}) copy-start(s32[64]{0:T(128)S(1)} %get-tuple-element.318) | copy-start | bytes 772 | tf_op jit(solution)/shard_map/while
  207.0 6.6 %copy-start.7 = (s32[64]{0:T(128)}, s32[64]{0:T(128)S(1)}, u32[]{:S(2)}) copy-start(s32[64]{0:T(128)S(1)} %get-tuple-element.318) | copy-start | bytes 772 | tf_op jit(solution)/shard_map/while
  224.7 6.6 %copy-start.7 = (s32[64]{0:T(128)}, s32[64]{0:T(128)S(1)}, u32[]{:S(2)}) copy-start(s32[64]{0:T(128)S(1)} %get-tuple-element.318) | copy-start | bytes 772 | tf_op jit(solution)/shard_map/while
  242.3 6.6 %copy-start.7 = (s32[64]{0:T(128)}, s32[64]{0:T(128)S(1)}, u32[]{:S(2)}) copy-start(s32[64]{0:T(128)S(1)} %get-tuple-element.318) | copy-start | bytes 772 | tf_op jit(solution)/shard_map/while
  260.0 6.6 %copy-start.7 = (s32[64]{0:T(128)}, s32[64]{0:T(128)S(1)}, u32[]{:S(2)}) copy-start(s32[64]{0:T(128)S(1)} %get-tuple-element.318) | copy-start | bytes 772 | tf_op jit(solution)/shard_map/while
  277.6 6.6 %copy-start.7 = (s32[64]{0:T(128)}, s32[64]{0:T(128)S(1)}, u32[]{:S(2)}) copy-start(s32[64]{0:T(128)S(1)} %get-tuple-element.318) | copy-start | bytes 772 | tf_op jit(solution)/shard_map/while
  295.3 6.6 %copy-start.7 = (s32[64]{0:T(128)}, s32[64]{0:T(128)S(1)}, u32[]{:S(2)}) copy-start(s32[64]{0:T(128)S(1)} %get-tuple-element.318) | copy-start | bytes 772 | tf_op jit(solution)/shard_map/while
  312.9 6.6 %copy-start.7 = (s32[64]{0:T(128)}, s32[64]{0:T(128)S(1)}, u32[]{:S(2)}) copy-start(s32[64]{0:T(128)S(1)} %get-tuple-element.318) | copy-start | bytes 772 | tf_op jit(solution)/shard_map/while
  330.6 6.6 %copy-start.7 = (s32[64]{0:T(128)}, s32[64]{0:T(128)S(1)}, u32[]{:S(2)}) copy-start(s32[64]{0:T(128)S(1)} %get-tuple-element.318) | copy-start | bytes 772 | tf_op jit(solution)/shard_map/while
  348.2 6.6 %copy-start.7 = (s32[64]{0:T(128)}, s32[64]{0:T(128)S(1)}, u32[]{:S(2)}) copy-start(s32[64]{0:T(128)S(1)} %get-tuple-element.318) | copy-start | bytes 772 | tf_op jit(solution)/shard_map/while
  365.9 6.6 %copy-start.7 = (s32[64]{0:T(128)}, s32[64]{0:T(128)S(1)}, u32[]{:S(2)}) copy-start(s32[64]{0:T(128)S(1)} %get-tuple-element.318) | copy-start | bytes 772 | tf_op jit(solution)/shard_map/while
  383.5 6.6 %copy-start.7 = (s32[64]{0:T(128)}, s32[64]{0:T(128)S(1)}, u32[]{:S(2)}) copy-start(s32[64]{0:T(128)S(1)} %get-tuple-element.318) | copy-start | bytes 772 | tf_op jit(solution)/shard_map/while
  401.2 6.6 %copy-start.7 = (s32[64]{0:T(128)}, s32[64]{0:T(128)S(1)}, u32[]{:S(2)}) copy-start(s32[64]{0:T(128)S(1)} %get-tuple-element.318) | copy-start | bytes 772 | tf_op jit(solution)/shard_map/while
  418.8 6.6 %copy-start.7 = (s32[64]{0:T(128)}, s32[64]{0:T(128)S(1)}, u32[]{:S(2)}) copy-start(s32[64]{0:T(128)S(1)} %get-tuple-element.318) | copy-start | bytes 772 | tf_op jit(solution)/shard_map/while
  436.5 6.6 %copy-start.7 = (s32[64]{0:T(128)}, s32[64]{0:T(128)S(1)}, u32[]{:S(2)}) copy-start(s32[64]{0:T(128)S(1)} %get-tuple-element.318) | copy-start | bytes 772 | tf_op jit(solution)/shard_map/while
  454.1 6.6 %copy-start.7 = (s32[64]{0:T(128)}, s32[64]{0:T(128)S(1)}, u32[]{:S(2)}) copy-start(s32[64]{0:T(128)S(1)} %get-tuple-element.318) | copy-start | bytes 772 | tf_op jit(solution)/shard_map/while
  471.8 6.6 %copy-start.7 = (s32[64]{0:T(128)}, s32[64]{0:T(128)S(1)}, u32[]{:S(2)}) copy-start(s32[64]{0:T(128)S(1)} %get-tuple-element.318) | copy-start | bytes 772 | tf_op jit(solution)/shard_map/while
  489.4 6.6 %copy-start.7 = (s32[64]{0:T(128)}, s32[64]{0:T(128)S(1)}, u32[]{:S(2)}) copy-start(s32[64]{0:T(128)S(1)} %get-tuple-element.318) | copy-start | bytes 772 | tf_op jit(solution)/shard_map/while
  508.7 76.9 %all-reduce.3.cloned.1.call-start = ((), (), s32[]{:S(2)}) async-start(), calls=%async_computation | async-start | bytes 524288 | tf_op jit(solution)/shard_map/psum | solution.py:125
  511.7 131.0 %copy-start.9 = (f32[32,1024]{1,0:T(8,128)S(1)}, f32[32,1024]{1,0:T(8,128)}, u32[]{:S(2)}) copy-start(f32[32,1024]{1,0:T(8,128)} %param.13) | copy-start | bytes 393220
  (119 other events, 388.3 us)
Sparse Core Ops, SparseCore 0:
  508.8 73.8 all-gather.1
Sparse Core Ops, SparseCore 1:
  511.5 33.0 all-reduce.2
